TPU v7x, 32 devices: a whole 2x2x4 slice. The times are simulated.
32 devices in a mesh: row: 8 (over z, y), col: 4 (over x, core).
Axes of the slice: x: 2, y: 2, z: 4, core: 2. Of those that a mesh axis runs over, the one named last changes fastest.
Arguments:
- front: float32 [8, 8, 128, 16, 4, 128], P(None, 'row', None, None, 'col'), as said below
- updates: float32 [2, 8, 8, 128, 12, 4, 128], P(None, None, 'row', None, None, 'col'), as said below
- maps: int32 [2, 48], replicated, may hold values from 0 to 63, as said below
Outputs:
- factor: float32 [8, 8, 128, 16, 4, 128], P(None, 'row', None, None, 'col')
Inputs may be any that keep to these rules, and one draw needn't show every extreme that they name: maps[k, j] is strictly increasing in j, and maps[k, j] - j is the same within each aligned group of 4 blocks. For each child and each c, of the blocks j with j % 4 == c at most 6 have maps[k, j] % 4 equal to any one value, and exactly 6 do for some value. updates[k] is child k's symmetric update matrix with its row block i placed at parent row block maps[k, i]; parent row blocks that no block of child k maps to are zero. front is symmetric, and with the updates added every block that is factored is positive definite.
All inputs are finite; a program needn't handle non-finite values.
Results may differ from a plain program's by a relative error of at most 0.0003.
Values sent between devices are 32-bit elements; how exact they have to be, the bound alone decides.
A program may use at most 192 MiB of HBM per device.

v0:
```python
import jax
import jax.numpy as jnp
from jax import lax
from jax.sharding import PartitionSpec as P

NP = 2


highest = lax.Precision.HIGHEST


def broadcast(value, axis, source):
    kept = jnp.where(lax.axis_index(axis) == source, value, 0).astype(value.dtype)
    return lax.psum(kept, axis)


def product(left_side, right_side):
    return jnp.dot(left_side, right_side, precision=highest, preferred_element_type=jnp.float32)


def routing(parent_of, col_count, child_cols, sources):
    block_ids = jnp.arange(child_cols, dtype=jnp.int32)
    child_ids = block_ids[None, :] * col_count + sources[:, None]
    lookup = child_ids[:, :, None] == jnp.arange(parent_of.shape[0], dtype=jnp.int32)[None, None, :]
    target = jnp.sum(jnp.where(lookup, parent_of[None, None, :], 0), axis=2)
    target_col = target % col_count
    target_slot = target // col_count
    by_col = target_col[:, :, None] == jnp.arange(col_count, dtype=jnp.int32)[None, None, :]
    running = jnp.cumsum(by_col.astype(jnp.int32), axis=1) - 1
    slot_rank = jnp.sum(jnp.where(by_col, running, 0), axis=2)
    return (target_col, slot_rank, target_slot)


def owner_rows(matrix, block_id, row_count, block_size, offset):
    root_row = block_id % row_count
    slot_index = block_id // row_count
    owned = matrix[slot_index * block_size : (slot_index + 1) * block_size, offset:]
    return broadcast(owned, "row", root_row)


def body(front, updates, maps):
    row_count = lax.axis_size("row")
    col_count = lax.axis_size("col")
    row_index = lax.axis_index("row")
    col_index = lax.axis_index("col")
    part_rows = front.shape[0]
    block_size = front.shape[2]
    part_cols = front.shape[3]
    child_cols = updates.shape[4]
    local_rows = part_rows * block_size
    local_cols = part_cols * block_size
    capacity = child_cols // 2
    panel_width = block_size * col_count
    col_ids = jnp.arange(col_count, dtype=jnp.int32)
    slot_ids = jnp.arange(capacity, dtype=jnp.int32)
    outgoing = []
    for member in range(2):
        target_col, slot_rank, target_slot = routing(
            maps[member], col_count, child_cols, jnp.reshape(col_index, (1,))
        )
        selector = (
            (target_col[0][None, None, :] == col_ids[:, None, None])
            & (slot_rank[0][None, None, :] == slot_ids[None, :, None])
        ).astype(jnp.float32)
        child_tiles = updates[member].reshape(local_rows, child_cols, block_size)
        outgoing.append(
            jnp.einsum(
                "qsb,rbj->qsrj",
                selector,
                child_tiles,
                precision=highest,
                preferred_element_type=jnp.float32,
            )
        )
    received = (
        lax.all_to_all(outgoing[0], "col", split_axis=0, concat_axis=0, tiled=True),
        lax.all_to_all(outgoing[1], "col", split_axis=0, concat_axis=0, tiled=True),
    )
    matrix = front.reshape(local_rows, part_cols, block_size)
    for member in range(2):
        target_col, slot_rank, target_slot = routing(maps[member], col_count, child_cols, col_ids)
        destined = target_col == col_index
        rank_hot = (
            (slot_rank[:, :, None] == slot_ids[None, None, :]) & destined[:, :, None]
        ).astype(jnp.float32)
        slot_hot = (
            target_slot[:, :, None] == jnp.arange(part_cols, dtype=jnp.int32)[None, None, :]
        ).astype(jnp.float32)
        placing = jnp.einsum(
            "ubs,ubp->usp",
            rank_hot,
            slot_hot,
            precision=highest,
            preferred_element_type=jnp.float32,
        )
        matrix = matrix + jnp.einsum(
            "usp,usrj->rpj",
            placing,
            received[member],
            precision=highest,
            preferred_element_type=jnp.float32,
        )
    matrix = matrix.reshape(local_rows, local_cols)
    row_global = (
        (jnp.arange(part_rows, dtype=jnp.int32)[:, None] * row_count + row_index) * block_size
        + jnp.arange(block_size, dtype=jnp.int32)[None, :]
    ).reshape(local_rows)
    col_global = (
        (jnp.arange(part_cols, dtype=jnp.int32)[:, None] * col_count + col_index) * block_size
        + jnp.arange(block_size, dtype=jnp.int32)[None, :]
    ).reshape(local_cols)
    identity = jnp.eye(panel_width, dtype=jnp.float32)
    for panel_index in range(NP):
        offset = panel_index * block_size
        begin_at = panel_index * panel_width
        finish = begin_at + panel_width
        column_piece = matrix[:, panel_index * block_size : (panel_index + 1) * block_size]
        panel_block = lax.all_gather(column_piece, "col", axis=1, tiled=True)
        top_rows = jnp.concatenate(
            [
                owner_rows(matrix, col_count * panel_index + quarter, row_count, block_size, offset)
                for quarter in range(col_count)
            ],
            axis=0,
        )
        diag_piece = top_rows[
            :, panel_index * block_size - offset : (panel_index + 1) * block_size - offset
        ]
        square = lax.all_gather(diag_piece, "col", axis=1, tiled=True)
        lower_factor = jnp.linalg.cholesky(square)
        inverse = lax.linalg.triangular_solve(lower_factor, identity, left_side=True, lower=True)
        left_factor = product(panel_block, inverse.T)
        beyond = row_global >= finish
        inside = (row_global >= begin_at) & (row_global < finish)
        masked_left = jnp.where(beyond[:, None], left_factor, 0.0)
        active_cols = col_global[offset:] >= finish
        right_factor = jnp.where(active_cols[None, :], product(inverse, top_rows), 0.0)
        trailing = product(masked_left, right_factor)
        matrix = matrix.at[:, offset:].add(-trailing)
        diag_rows = lower_factor[jnp.clip(row_global - begin_at, 0, panel_width - 1)]
        column_vals = jnp.where(
            beyond[:, None], left_factor, jnp.where(inside[:, None], diag_rows, 0.0)
        )
        own_cols = lax.dynamic_slice_in_dim(column_vals, col_index * block_size, block_size, 1)
        matrix = matrix.at[:, panel_index * block_size : (panel_index + 1) * block_size].set(
            own_cols
        )
        matrix = jnp.where(inside[:, None] & (col_global >= finish)[None, :], 0.0, matrix)
    return matrix.reshape(front.shape)


def solution(mesh):
    return jax.shard_map(
        body,
        mesh=mesh,
        in_specs=(
            P(None, "row", None, None, "col", None),
            P(None, None, "row", None, None, "col", None),
            P(),
        ),
        out_specs=P(None, "row", None, None, "col", None),
        check_vma=False,
    )
```

profile of v0, /device:TPU:0, one launch (start us, length us, event | category | flops | bytes accessed | tf_op | source)
XLA Modules:
  0.0 1142.8 jit_solution(502032055273799692)
XLA Ops:
  8.4 11.1 fusion.140
  20.2 12.2 %fusion.90 = f32[4,6,1024,128]{3,1,2,0:T(8,128)} fusion(f32[1024,12,128,1]{2,1,0,3:T(8,128)S(1)} %bitcast.179, pred[6,12]{1,0:T(8,128)(4,1)S(1)} %iota_compare_fusion.13, pred[4,12]{1,0:T(4,128)(4,1)S(1)} %iota_compare_fusion.16), kind=kOutput, calls=%fused_computation.176 | convolution fusion | flops 452985120 | bytes 18874488 | tf_op jit(solution)/shard_map/qsb,rbj->qsrj/dot_general | solution.py:67
  32.4 12.4 %copy.102 = f32[4,6,1024,128]{3,2,1,0:T(8,128)} copy(f32[4,6,1024,128]{3,1,2,0:T(8,128)} %fusion.90) | data formatting | bytes 25165824 | tf_op jit(solution)/shard_map/qsb,rbj->qsrj/dot_general | solution.py:67
  44.8 6.5 all-to-all-start.1
  51.4 3.5 copy.138
  54.9 12.2 %fusion.92 = f32[4,6,1024,128]{3,1,2,0:T(8,128)} fusion(f32[1024,12,128,1]{2,1,0,3:T(8,128)S(1)} %bitcast.178, pred[6,12]{1,0:T(8,128)(4,1)S(1)} %iota_compare_fusion.14, pred[4,12]{1,0:T(4,128)(4,1)S(1)} %iota_compare_fusion.18), kind=kOutput, calls=%fused_computation.178 | convolution fusion | flops 452985120 | bytes 18874488 | tf_op jit(solution)/shard_map/qsb,rbj->qsrj/dot_general | solution.py:67
  67.1 12.5 %copy.94 = f32[4,6,1024,128]{3,2,1,0:T(8,128)} copy(f32[4,6,1024,128]{3,1,2,0:T(8,128)} %fusion.92) | data formatting | bytes 25165824 | tf_op jit(solution)/shard_map/qsb,rbj->qsrj/dot_general | solution.py:67
  79.6 110.4 %all-to-all-done.1 = f32[4,6,1024,128]{3,2,1,0:T(8,128)} async-done(((f32[4,6,1024,128]{3,2,1,0:T(8,128)}), f32[4,6,1024,128]{3,2,1,0:T(8,128)}, u32[]{:S(2)}, u32[]{:S(2)}) %all-to-all-start.1) | async-done | bytes 12582944 | tf_op jit(solution)/shard_map/all_to_all | solution.py:77
  190.0 6.3 all-to-all-start
  199.6 28.3 %fusion = f32[1024,128,16,1]{1,2,3,0:T(8,128)} fusion(f32[4,6,16,1]{2,1,0,3:T(8,128)S(1)} %convolution_bitcast_fusion, f32[4,6,1024,128]{3,2,1,0:T(8,128)} %all-to-all-done.1), kind=kOutput, calls=%fused_computation.6 | convolution fusion | flops 603979776 | bytes 20973056 | tf_op jit(solution)/shard_map/usp,usrj->rpj/dot_general | solution.py:96
  227.9 106.6 %all-to-all-done = f32[4,6,1024,128]{3,2,1,0:T(8,128)} async-done(((f32[4,6,1024,128]{3,2,1,0:T(8,128)}), f32[4,6,1024,128]{3,2,1,0:T(8,128)}, u32[]{:S(2)}, u32[]{:S(2)}) %all-to-all-start) | async-done | bytes 12582944 | tf_op jit(solution)/shard_map/all_to_all | solution.py:76
  334.5 31.0 %bitcast_add_fusion = f32[1024,16,128]{2,1,0:T(8,128)S(1)} fusion(f32[1024,128,16,1]{1,2,3,0:T(8,128)} %fusion, f32[1024,16,128]{2,1,0:T(8,128)} %bitcast.181, f32[4,6,16,1]{2,1,0,3:T(8,128)S(1)} %convolution_bitcast_fusion.1, f32[4,6,1024,128]{3,2,1,0:T(8,128)} %all-to-all-done), kind=kOutput, calls=%fused_computation.10 | convolution fusion | flops 608174080 | bytes 37750272 | tf_op jit(solution)/shard_map/usp,usrj->rpj/dot_general | solution.py:96
  365.5 3.4 copy-done.1
  368.9 1.8 slice_select_fusion
  370.6 2.7 copy.109
  373.3 2.6 copy.110
  379.4 158.1 %all-reduce.8.cloned.1.call-done = (f32[128,2048]{0,1:T(8,128)}, f32[128,2048]{0,1:T(8,128)}, f32[128,2048]{0,1:T(8,128)}, f32[128,2048]{0,1:T(8,128)}) async-done(((f32[128,2048]{0,1:T(8,128)}, f32[128,2048]{0,1:T(8,128)}, f32[128,2048]{0,1:T(8,128)}, f32[128,2048]{0,1:T(8,128)}), (f32[128,2048]{0,1:T(8,128)}, f32[128,2048]{0,1:T(8,128)}, f32[128,2048]{0,1:T(8,128)}, ...) | async-done | bytes 4194320 | tf_op jit(solution)/shard_map/psum | solution.py:14
  540.7 2.0 copy-done.4
  543.9 8.8 copy.108
  552.7 1.9 slice.270
  555.1 4.1 all-gather.7.cloned.1.call-done
  563.2 11.7 %cholesky.286 = f32[128,128]{1,0:T(8,128)S(1)} custom-call(f32[128,128]{1,0:T(8,128)S(1)} %cholesky.426), custom_call_target="Cholesky" | custom-call | tf_op jit(solution)/shard_map/jit(cholesky)/cholesky | solution.py:130
  575.1 9.8 custom-call.27
  587.4 11.7 %cholesky.305 = f32[128,128]{1,0:T(8,128)S(1)} custom-call(f32[128,128]{1,0:T(8,128)S(1)} %cholesky.430), custom_call_target="Cholesky" | custom-call | tf_op jit(solution)/shard_map/jit(cholesky)/cholesky | solution.py:130
  600.4 10.0 custom-call.28
  612.0 11.7 %cholesky.326 = f32[128,128]{1,0:T(8,128)S(1)} custom-call(f32[128,128]{1,0:T(8,128)S(1)} %cholesky.435), custom_call_target="Cholesky" | custom-call | tf_op jit(solution)/shard_map/jit(cholesky)/cholesky | solution.py:130
  624.4 9.8 custom-call.29
  635.6 11.7 %cholesky.343 = f32[128,128]{1,0:T(8,128)S(1)} custom-call(f32[128,128]{1,0:T(8,128)S(1)} %convolution_subtract_fusion.11), custom_call_target="Cholesky" | custom-call | tf_op jit(solution)/shard_map/jit(cholesky)/cholesky | solution.py:130
  652.0 11.5 %while.9 = (s32[]{:T(128)}, f32[512,512]{1,0:T(8,128)}, s32[4,2]{0,1:T(2,128)S(1)}, f32[4,128,128]{2,1,0:T(8,128)S(1)}, s32[]{:T(128)}) while((s32[]{:T(128)}, f32[512,512]{1,0:T(8,128)}, s32[4,2]{0,1:T(2,128)S(1)}, f32[4,128,128]{2,1,0:T(8,128)S(1)}, s32[]{:T(128)}) %tuple.92), condition=%wide.while_cond.4, body=%wide.while_body.4.sunk | while | flops 2 | bytes 131181 | solution.py:131
  652.6 2.3 bitcast_dynamic-update-slice_fusion.4
  655.5 2.3 bitcast_dynamic-update-slice_fusion.4
  658.4 2.3 bitcast_dynamic-update-slice_fusion.4
  661.3 2.2 bitcast_dynamic-update-slice_fusion.4
  663.5 39.3 %custom-call.30 = f32[4,128,128]{1,2,0:T(8,128)S(1)} custom-call(f32[4,128,128]{2,1,0:T(8,128)S(1)} %get-tuple-element.77), custom_call_target="InvertDiagBlocksLowerTriangular" | custom-call | tf_op jit(solution)/shard_map/triangular_solve/custom-call.3 | solution.py:131
  702.8 4.9 gather_fusion
  715.0 8.5 fusion.36
  723.5 5.3 fusion.37
  728.8 16.5 %negate_add_fusion = f32[1024,2048]{0,1:T(8,128)S(1)} fusion(f32[1024,2048]{0,1:T(8,128)} %bitcast.177, f32[512,2048]{1,0:T(8,128)S(1)} %copy-done.2, f32[1024,512]{0,1:T(8,128)S(1)} %fusion.37, pred[2048]{0:T(1024)(128)(4,1)S(1)} %get-tuple-element.152, pred[1024]{0:T(1024)(128)(4,1)S(1)} %get-tuple-element.157), kind=kOutput, calls=%fused_computation.13 | convolution fusion | flops 12890669056 | bytes 23071744 | tf_op jit(solution)/shard_map/dot_general | solution.py:18
  747.1 3.4 copy-done
  750.5 2.0 slice_select_fusion.4
  752.6 150.5 %all-reduce.6.cloned.1.call-done = (f32[128,1920]{0,1:T(8,128)}, f32[128,1920]{0,1:T(8,128)}, f32[128,1920]{0,1:T(8,128)}, f32[128,1920]{0,1:T(8,128)}) async-done(((f32[128,1920]{0,1:T(8,128)}, f32[128,1920]{0,1:T(8,128)}, f32[128,1920]{0,1:T(8,128)}, f32[128,1920]{0,1:T(8,128)}), (f32[128,1920]{0,1:T(8,128)}, f32[128,1920]{0,1:T(8,128)}, f32[128,1920]{0,1:T(8,128)}, ...) | async-done | bytes 3932176 | tf_op jit(solution)/shard_map/psum | solution.py:14
  906.3 1.9 copy-done.6
  910.0 1.9 slice.286
  911.9 12.8 %all-gather.11.cloned.1.call-done = f32[512,512]{0,1:T(8,128)} async-done(((f32[512,128]{0,1:T(8,128)}), f32[512,512]{0,1:T(8,128)}) %all-gather.11.cloned.1.call-update) | async-done | bytes 1048592 | tf_op jit(solution)/shard_map/all_gather | solution.py:129
  928.7 11.7 %cholesky.358 = f32[128,128]{1,0:T(8,128)S(1)} custom-call(f32[128,128]{1,0:T(8,128)S(1)} %cholesky.439), custom_call_target="Cholesky" | custom-call | tf_op jit(solution)/shard_map/jit(cholesky)/cholesky | solution.py:130
  940.6 9.8 custom-call.31
  952.9 11.7 %cholesky.377 = f32[128,128]{1,0:T(8,128)S(1)} custom-call(f32[128,128]{1,0:T(8,128)S(1)} %cholesky.443), custom_call_target="Cholesky" | custom-call | tf_op jit(solution)/shard_map/jit(cholesky)/cholesky | solution.py:130
  966.0 10.2 custom-call.32
  977.7 11.7 %cholesky.398 = f32[128,128]{1,0:T(8,128)S(1)} custom-call(f32[128,128]{1,0:T(8,128)S(1)} %cholesky.448), custom_call_target="Cholesky" | custom-call | tf_op jit(solution)/shard_map/jit(cholesky)/cholesky | solution.py:130
  990.1 9.8 custom-call.33
  1001.4 11.7 %cholesky.415 = f32[128,128]{1,0:T(8,128)S(1)} custom-call(f32[128,128]{1,0:T(8,128)S(1)} %convolution_subtract_fusion.10), custom_call_target="Cholesky" | custom-call | tf_op jit(solution)/shard_map/jit(cholesky)/cholesky | solution.py:130
  1017.7 11.5 %while.10 = (s32[]{:T(128)}, f32[512,512]{1,0:T(8,128)}, s32[4,2]{0,1:T(2,128)S(1)}, f32[4,128,128]{2,1,0:T(8,128)S(1)}, s32[]{:T(128)}) while((s32[]{:T(128)}, f32[512,512]{1,0:T(8,128)}, s32[4,2]{0,1:T(2,128)S(1)}, f32[4,128,128]{2,1,0:T(8,128)S(1)}, s32[]{:T(128)}) %tuple.112), condition=%wide.while_cond.4.clone, body=%wide.while_body.4.clone.sunk | while | flops 2 | bytes 131181 | solution.py:131
  1018.3 2.3 bitcast_dynamic-update-slice_fusion.5
  1021.2 2.3 bitcast_dynamic-update-slice_fusion.5
  1024.1 2.3 bitcast_dynamic-update-slice_fusion.5
  1027.0 2.2 bitcast_dynamic-update-slice_fusion.5
  1029.2 39.3 %custom-call.34 = f32[4,128,128]{1,2,0:T(8,128)S(1)} custom-call(f32[4,128,128]{2,1,0:T(8,128)S(1)} %get-tuple-element.78), custom_call_target="InvertDiagBlocksLowerTriangular" | custom-call | tf_op jit(solution)/shard_map/triangular_solve/custom-call.3 | solution.py:131
  1068.5 4.9 gather_fusion.1
  1080.8 8.7 fusion.34
  1089.5 5.5 fusion.35
  1095.0 16.8 %constant_dynamic-update-slice_fusion.9 = (f32[1024,2048]{0,1:T(8,128)}, f32[1024,1920]{0,1:T(8,128)S(1)}) fusion(f32[1024,2048]{0,1:T(8,128)} %copy-done, f32[512,1920]{1,0:T(8,128)S(1)} %copy-done.3, pred[1920]{0:T(1024)(128)(4,1)S(1)} %fusion.100, f32[1024,512]{0,1:T(8,128)S(1)} %fusion.35, pred[1024]{0:T(1024)(128)(4,1)S(1)} %get-tuple-element.155), kind=kOutput, calls=%fused_computation.234 | convolution fusion | flops 12085035008 | bytes 29625216 | tf_op jit(solution)/shard_map/dot_general | solution.py:18
  1113.4 4.0 select_bitcast_fusion
  1117.4 5.3 copy.142
  1122.7 13.1 %copy.123 = f32[8,1,128,16,1,128]{5,4,3,2,1,0:T(1,128)} copy(f32[8,1,128,16,1,128]{2,0,5,3,4,1:T(8,128)} %bitcast.180) | data formatting | bytes 16777216 | tf_op jit(solution)/shard_map/reshape | solution.py:149
  (180 shorter events, 69.2 us)
Async XLA Ops:
  44.8 145.2 %all-to-all-start.1 = ((f32[4,6,1024,128]{3,2,1,0:T(8,128)}), f32[4,6,1024,128]{3,2,1,0:T(8,128)}, u32[]{:S(2)}, u32[]{:S(2)}) async-start(f32[4,6,1024,128]{3,2,1,0:T(8,128)} %copy.102), calls=%async_computation.1 | async-start | bytes 25165824 | tf_op jit(solution)/shard_map/all_to_all | solution.py:77
  190.0 144.5 %all-to-all-start = ((f32[4,6,1024,128]{3,2,1,0:T(8,128)}), f32[4,6,1024,128]{3,2,1,0:T(8,128)}, u32[]{:S(2)}, u32[]{:S(2)}) async-start(f32[4,6,1024,128]{3,2,1,0:T(8,128)} %copy.94), calls=%async_computation | async-start | bytes 25165824 | tf_op jit(solution)/shard_map/all_to_all | solution.py:76
  196.4 341.1 %all-reduce.8.cloned.1.call-start = ((), (), s32[]{:S(2)}) async-start(), calls=%async_computation.7 | async-start | bytes 8388608 | tf_op jit(solution)/shard_map/psum | solution.py:14
  365.5 3.4 copy-start.1
  370.6 5.3 copy-start.8
  378.8 180.4 %all-gather.7.cloned.1.call-start = ((), (), s32[]{:S(2)}) async-start(), calls=%async_computation.3 | async-start | bytes 1310720 | tf_op jit(solution)/shard_map/all_gather | solution.py:129
  537.5 2.9 copy-start.12
  537.5 3.0 copy-start.11
  540.7 2.0 copy-start.4
  543.4 180.1 %all-gather.5.cloned.1.call-start = ((), (), s32[]{:S(2)}) async-start(), calls=%async_computation.2 | async-start | bytes 2621440 | tf_op jit(solution)/shard_map/all_gather | solution.py:118
  554.6 348.5 %all-reduce.6.cloned.1.call-start = ((), (), s32[]{:S(2)}) async-start(), calls=%async_computation.6 | async-start | bytes 7864320 | tf_op jit(solution)/shard_map/psum | solution.py:14
  562.2 1.0 copy-start.9
  709.0 6.1 copy-start.5
  723.5 5.3 copy-start.2
  747.1 3.4 copy-start
  752.6 172.1 %all-gather.11.cloned.1.call-start = ((), (), s32[]{:S(2)}) async-start(), calls=%async_computation.5 | async-start | bytes 1310720 | tf_op jit(solution)/shard_map/all_gather | solution.py:129
  903.1 2.8 copy-start.14
  903.1 3.0 copy-start.13
  906.2 1.9 copy-start.6
  908.9 180.6 %all-gather.9.cloned.1.call-start = ((), (), s32[]{:S(2)}) async-start(), calls=%async_computation.4 | async-start | bytes 2621440 | tf_op jit(solution)/shard_map/all_gather | solution.py:118
  927.7 1.0 copy-start.10
  1074.7 6.1 copy-start.7
  1089.5 5.5 copy-start.3
Sparse Core Ops, SparseCore 0:
  378.9 158.5 all-reduce.7
  543.6 15.5 all-gather.6
  560.7 22.6 all-gather.4
  752.7 150.4 all-reduce.5
  909.0 15.6 all-gather.10
  926.1 22.6 all-gather.8
where the time goes:
time: 1150 us; the launch traced here: 1140 us
  waiting for transfers between devices  543 us (47%)
  other arithmetic  259 us (23%)
  matrix products  168 us (15%)
  local copies, waits for them, and re-layouts  139 us (12%)
  between operations  19.6 us (2%)
  starting transfers between devices  13.9 us (1%)
    psum x2, waiting for transfers between devices, broadcast(): return lax.psum(kept, axis)  309 us
    another operation x30, other arithmetic, body(): lower_factor = jnp.linalg.cholesky(square)  159 us
    all_to_all x1, waiting for transfers between devices, body(): lax.all_to_all(outgoing[1], 'col', split_axis=0, concat_axis=0, tiled=True)  110 us
    all_to_all x1, waiting for transfers between devices, body(): lax.all_to_all(outgoing[0], 'col', split_axis=0, concat_axis=0, tiled=True)  107 us
    another operation x5, other arithmetic, body(): lax.linalg.triangular_solve(lower_factor, identity, left_side=True, lower...  81.4 us
    dot_general x6, matrix products, product(): jnp.dot(left_side, right_side, precision=highest, preferred_element_type=...  61.3 us
    dot_general x2, matrix products, body(): jnp.einsum('usp,usrj->rpj', placing, received[member], precision=highest,...  59.3 us
    dot_general x2, local copies, waits for them, and re-layouts, body(): jnp.einsum('qsb,rbj->qsrj', selector, child_tiles, precision=highest, pre...  25 us
  transfers between devices with their start and end apart: 8, of which 6 were waited for; matrix products, arithmetic and copies ran while one was open for 35% of the time, Pallas kernels for 0%

commit v1 on v0

v1 whole, which is shorter than its diff:
```python
import functools

import jax
import jax.numpy as jnp
from jax import lax
from jax.experimental import pallas as pl
from jax.experimental.pallas import tpu as pltpu
from jax.sharding import PartitionSpec as P

NP = 2
highest = lax.Precision.HIGHEST
VMEM_LIMIT = 56 * 1024 * 1024


def split(value):
    high = value.astype(jnp.bfloat16)
    low = (value - high.astype(jnp.float32)).astype(jnp.bfloat16)
    return high, low


def dims(transposed):
    return (((1,), (1 if transposed else 0,)), ((), ()))


def product3(left_pair, right_pair, transposed=False):
    def one(a, b):
        return lax.dot_general(a, b, dims(transposed), preferred_element_type=jnp.float32)

    return (
        one(left_pair[0], right_pair[0])
        + one(left_pair[0], right_pair[1])
        + one(left_pair[1], right_pair[0])
    )


def product(a, b, transposed=False):
    return lax.dot_general(
        a, b, dims(transposed), precision=highest, preferred_element_type=jnp.float32
    )


def pack_kernel(child_cols, cap, blk, table, updates_ref, one_ref, two_ref, three_ref):
    for turn, out_ref in enumerate((one_ref, two_ref, three_ref)):
        for member in range(2):
            for slot in range(cap):
                source = table[(turn + 1) * 2 * cap + member * cap + slot]
                out_ref[member * cap + slot] = updates_ref[
                    member, 0, pl.ds(source, blk, stride=child_cols), :
                ]


def pack(table, updates, cap):
    part_rows, blk, child_cols = updates.shape[1], updates.shape[3], updates.shape[4]
    flat = updates.reshape(2, part_rows, blk * child_cols, blk)
    return pl.pallas_call(
        functools.partial(pack_kernel, child_cols, cap, blk),
        grid_spec=pltpu.PrefetchScalarGridSpec(
            num_scalar_prefetch=1,
            grid=(part_rows,),
            in_specs=[pl.BlockSpec((2, 1, blk * child_cols, blk), lambda a, t: (0, a, 0, 0))],
            out_specs=[pl.BlockSpec((2 * cap, blk, blk), lambda a, t: (0, a, 0))] * 3,
        ),
        out_shape=[jax.ShapeDtypeStruct((2 * cap, part_rows * blk, blk), jnp.float32)] * 3,
        compiler_params=pltpu.CompilerParams(vmem_limit_bytes=VMEM_LIMIT),
        name="pack",
    )(table, flat)


def assemble_kernel(part_cols, child_cols, blk, table, front_ref, updates_ref, *refs):
    received, out_ref = refs[:3], refs[3]
    for slot in range(part_cols):
        cols = slice(slot * blk, (slot + 1) * blk)
        out_ref[:, cols] = front_ref[0, pl.ds(slot, blk, stride=part_cols), :]
        for member in range(2):
            turn = table[(member * part_cols + slot) * 2]
            index = table[(member * part_cols + slot) * 2 + 1]

            @pl.when(turn == 0)
            def _():
                out_ref[:, cols] += updates_ref[member, 0, pl.ds(index, blk, stride=child_cols), :]

            for step in range(3):

                @pl.when(turn == step + 1)
                def _():
                    out_ref[:, cols] += received[step][index]


def assemble(table, front, updates, received):
    part_rows, blk, part_cols = front.shape[0], front.shape[2], front.shape[3]
    child_cols = updates.shape[4]
    slots = received[0].shape[0]
    return pl.pallas_call(
        functools.partial(assemble_kernel, part_cols, child_cols, blk),
        grid_spec=pltpu.PrefetchScalarGridSpec(
            num_scalar_prefetch=1,
            grid=(part_rows,),
            in_specs=[
                pl.BlockSpec((1, blk * part_cols, blk), lambda a, t: (a, 0, 0)),
                pl.BlockSpec((2, 1, blk * child_cols, blk), lambda a, t: (0, a, 0, 0)),
            ]
            + [pl.BlockSpec((slots, blk, blk), lambda a, t: (0, a, 0))] * 3,
            out_specs=pl.BlockSpec((blk, part_cols * blk), lambda a, t: (a, 0)),
        ),
        out_shape=jax.ShapeDtypeStruct((part_rows * blk, part_cols * blk), jnp.float32),
        compiler_params=pltpu.CompilerParams(vmem_limit_bytes=VMEM_LIMIT),
        name="assemble",
    )(
        table,
        front.reshape(part_rows, blk * part_cols, blk),
        updates.reshape(2, part_rows, blk * child_cols, blk),
        *received,
    )


def eliminate(block):
    size = block.shape[0]
    row_ids = lax.broadcasted_iota(jnp.int32, (size, size), 0)
    col_ids = lax.broadcasted_iota(jnp.int32, (size, size), 1)
    tiles = size // 8
    upper = [block[8 * t : 8 * t + 8, :] for t in range(tiles)]
    start = (row_ids == col_ids).astype(jnp.float32)
    solved = [start[8 * t : 8 * t + 8, :] for t in range(tiles)]
    local = lax.broadcasted_iota(jnp.int32, (8, size), 0)
    for j in range(size):
        home, inner = j // 8, j % 8
        pivot_row = upper[home][inner : inner + 1, :]
        solved_row = solved[home][inner : inner + 1, :]
        scale = 1.0 / pivot_row[:, j : j + 1]
        for t in range(home, tiles):
            if t == home and inner == 7:
                continue
            factor = upper[t][:, j : j + 1] * scale
            if t == home:
                factor = jnp.where(local[:, :1] > inner, factor, 0.0)
            upper[t] = upper[t] - factor * pivot_row
            solved[t] = solved[t] - factor * solved_row
    upper = jnp.concatenate(upper, axis=0)
    solved = jnp.concatenate(solved, axis=0)
    diagonal = jnp.sum(jnp.where(row_ids == col_ids, upper, 0.0), axis=1, keepdims=True)
    scale = 1.0 / jnp.sqrt(diagonal)
    lower = jnp.where(col_ids >= row_ids, upper * scale, 0.0).T
    return lower, solved * scale


def factor_kernel(blk, square_ref, lower_ref, inverse_ref, work):
    size = square_ref.shape[0]
    count = size // blk
    work[...] = square_ref[...]
    lower_ref[...] = jnp.zeros_like(lower_ref)
    inverse_ref[...] = jnp.zeros_like(inverse_ref)
    rows = lax.broadcasted_iota(jnp.int32, (size, blk), 0)

    def step(k, carry):
        begin = pl.multiple_of(k * blk, blk)
        here = pl.ds(begin, blk)
        diag_lower, diag_inverse = eliminate(work[here, here])
        inverse_ref[here, here] = diag_inverse
        column = product(work[:, here], diag_inverse, True)
        column = jnp.where(rows >= begin + blk, column, 0.0)
        lower_ref[:, here] = column
        lower_ref[here, here] = diag_lower
        for q in range(0, size, 256):
            piece = slice(q, q + 256)

            @pl.when(q + 256 > begin + blk)
            def _():
                work[piece, :] -= product(lower_ref[piece, here] * (rows[piece] >= begin + blk), column, True)

        return carry

    lax.fori_loop(0, count, step, 0)

    def substitute(i, carry):
        begin = pl.multiple_of(i * blk, blk)
        here = pl.ds(begin, blk)
        cols = lax.broadcasted_iota(jnp.int32, (blk, size), 1)
        diag_inverse = inverse_ref[here, here]
        strip = jnp.where(cols < begin, lower_ref[here, :], 0.0)
        total = product(strip, inverse_ref[...])
        update = product(diag_inverse, total)
        inverse_ref[here, :] -= update
        return carry

    lax.fori_loop(1, count, substitute, 0)


def factorize(square, blk):
    size = square.shape[0]
    shape = jax.ShapeDtypeStruct((size, size), jnp.float32)
    return pl.pallas_call(
        functools.partial(factor_kernel, blk),
        out_shape=[shape, shape],
        scratch_shapes=[pltpu.VMEM((size, size), jnp.float32)],
        compiler_params=pltpu.CompilerParams(vmem_limit_bytes=VMEM_LIMIT),
        name="factorize",
    )(square)


def right_kernel(inverse_ref, top_ref, high_ref, low_ref, inv_high, inv_low):
    @pl.when(pl.program_id(0) == 0)
    def _():
        inv_high[...], inv_low[...] = split(inverse_ref[...])

    result = product3((inv_high[...], inv_low[...]), split(top_ref[...]))
    high_ref[...], low_ref[...] = split(result)


def right_side(inverse, top, skip, tile):
    size, cols = top.shape
    out = jax.ShapeDtypeStruct((size, cols - skip), jnp.bfloat16)
    return pl.pallas_call(
        right_kernel,
        grid=((cols - skip) // tile,),
        in_specs=[
            pl.BlockSpec((size, size), lambda n: (0, 0)),
            pl.BlockSpec((size, tile), lambda n: (0, n + skip // tile)),
        ],
        out_specs=[pl.BlockSpec((size, tile), lambda n: (0, n))] * 2,
        out_shape=[out, out],
        scratch_shapes=[pltpu.VMEM((size, size), jnp.bfloat16)] * 2,
        compiler_params=pltpu.CompilerParams(vmem_limit_bytes=VMEM_LIMIT),
        name="right",
    )(inverse, top)


def final_kernel(
    part_cols, blk, row_count, col_count, place,
    panel_ref, matrix_ref, inverse_ref, lower_ref, high_ref, low_ref,
    out_ref, inv_high, inv_low, left_ref,
):
    step = pl.program_id(0)
    row_blocks = out_ref.shape[0]
    panel_blocks = NP * col_count

    @pl.when(step == 0)
    def _():
        inv_high[...], inv_low[...] = split(inverse_ref[...])

    left_ref[...] = product3(split(panel_ref[...]), (inv_high[...], inv_low[...]), True)
    left_pair = split(left_ref[...])
    for pair in range(NP, part_cols, 2):
        cols = slice((pair - NP) * blk, (pair - NP + 2) * blk)
        trailing = product3(left_pair, (high_ref[:, cols], low_ref[:, cols]))
        updated = matrix_ref[:, pair * blk : (pair + 2) * blk] - trailing
        for t in range(row_blocks):
            for half in range(2):
                out_ref[t, pl.ds(pair + half, blk, stride=part_cols), :] = updated[
                    t * blk : (t + 1) * blk, half * blk : (half + 1) * blk
                ]
    for t in range(row_blocks):
        block_row = (step * row_blocks + t) * row_count + place[0]
        for slot in range(NP):
            start = pl.multiple_of((slot * col_count + place[1]) * blk, blk)
            out_ref[t, pl.ds(slot, blk, stride=part_cols), :] = left_ref[
                t * blk : (t + 1) * blk, pl.ds(start, blk)
            ]

        @pl.when(block_row < panel_blocks)
        def _():
            out_ref[t] = jnp.zeros_like(out_ref[t])
            begin = pl.multiple_of(block_row * blk, blk)
            for slot in range(NP):
                start = pl.multiple_of((slot * col_count + place[1]) * blk, blk)
                out_ref[t, pl.ds(slot, blk, stride=part_cols), :] = lower_ref[
                    pl.ds(begin, blk), pl.ds(start, blk)
                ]


def finish(place, panel, matrix, inverse, lower, high, low, row_count, col_count, blk):
    rows, cols = matrix.shape
    part_rows, part_cols = rows // blk, cols // blk
    size = inverse.shape[0]
    group = 2 if part_rows % 2 == 0 else 1

    def resident(shape):
        return pl.BlockSpec(shape, lambda a, t: (0, 0), pipeline_mode=pl.Buffered(1))

    def kernel(place, *refs):
        final_kernel(part_cols, blk, row_count, col_count, place, *refs)

    return pl.pallas_call(
        kernel,
        grid_spec=pltpu.PrefetchScalarGridSpec(
            num_scalar_prefetch=1,
            grid=(part_rows // group,),
            in_specs=[
                pl.BlockSpec((group * blk, size), lambda a, t: (a, 0)),
                pl.BlockSpec((group * blk, cols), lambda a, t: (a, 0)),
                resident((size, size)),
                resident((size, size)),
                resident(high.shape),
                resident(low.shape),
            ],
            out_specs=pl.BlockSpec((group, blk * part_cols, blk), lambda a, t: (a, 0, 0)),
            scratch_shapes=[
                pltpu.VMEM((size, size), jnp.bfloat16),
                pltpu.VMEM((size, size), jnp.bfloat16),
                pltpu.VMEM((group * blk, size), jnp.float32),
            ],
        ),
        out_shape=jax.ShapeDtypeStruct((part_rows, blk * part_cols, blk), jnp.float32),
        compiler_params=pltpu.CompilerParams(vmem_limit_bytes=VMEM_LIMIT),
        name="finish",
    )(place, panel, matrix, inverse, lower, high, low)


def tables(maps, col_index, col_count, child_cols, part_cols, cap):
    offsets = maps[:, ::col_count] - col_count * jnp.arange(child_cols, dtype=jnp.int32)[None, :]
    turn = offsets % col_count
    groups = jnp.arange(child_cols, dtype=jnp.int32)
    same = (turn[:, :, None] == turn[:, None, :]) & (groups[None, None, :] < groups[None, :, None])
    rank = jnp.sum(same.astype(jnp.int32), axis=2)
    turns = jnp.arange(col_count, dtype=jnp.int32)
    slots = jnp.arange(cap, dtype=jnp.int32)
    hot = (turn[None, :, None, :] == turns[:, None, None, None]) & (
        rank[None, :, None, :] == slots[None, None, :, None]
    )
    send = jnp.sum(jnp.where(hot, groups[None, None, None, :], 0), axis=3).reshape(-1)
    parents = jnp.arange(part_cols, dtype=jnp.int32) * col_count + col_index
    match = maps[:, None, :] == parents[None, :, None]
    spread = jnp.repeat(groups, col_count)
    group = jnp.sum(jnp.where(match, spread[None, None, :], 0), axis=2)
    present = jnp.any(match, axis=2)
    pick = group[:, :, None] == groups[None, None, :]
    kind = jnp.sum(jnp.where(pick, turn[:, None, :], 0), axis=2)
    order = jnp.sum(jnp.where(pick, rank[:, None, :], 0), axis=2)
    order = jnp.where(kind == 0, group, order + cap * jnp.arange(2, dtype=jnp.int32)[:, None])
    kind = jnp.where(present, kind, col_count)
    place = jnp.stack([kind, order], axis=2).reshape(-1)
    return send, place


def gather_top(piece, row_count, row_index, panel_blocks):
    if row_count == panel_blocks:
        return lax.all_gather(piece, "row", axis=0, tiled=True)
    ids = jnp.arange(panel_blocks, dtype=jnp.int32)
    kept = jnp.where((ids == row_index)[:, None, None], piece[None], 0.0)
    return lax.psum(kept, "row").reshape(panel_blocks * piece.shape[0], piece.shape[1])


def body(front, updates, maps):
    row_count = lax.axis_size("row")
    col_count = lax.axis_size("col")
    row_index = lax.axis_index("row")
    col_index = lax.axis_index("col")
    front = front.reshape(front.shape[0], 1, *front.shape[2:4], front.shape[5])
    blk, part_cols = front.shape[2], front.shape[3]
    child_cols = updates.shape[4]
    cap = child_cols // 2
    panel_blocks = NP * col_count
    send, place = tables(maps, col_index, col_count, child_cols, part_cols, cap)
    outgoing = pack(send, updates, cap)
    received = []
    for turn in range(1, col_count):
        pairs = [(c, (c + turn) % col_count) for c in range(col_count)]
        received.append(lax.ppermute(outgoing[turn - 1], "col", pairs))
    matrix = assemble(place, front, updates, received)
    panel = jnp.concatenate(
        [
            lax.all_gather(matrix[:, s * blk : (s + 1) * blk], "col", axis=1, tiled=True)
            for s in range(NP)
        ],
        axis=1,
    )
    top = gather_top(matrix[:blk], row_count, row_index, panel_blocks)
    square = gather_top(panel[:blk], row_count, row_index, panel_blocks)
    lower, inverse = factorize(square, blk)
    high, low = right_side(inverse, top, NP * blk, 2 * blk)
    where = jnp.stack([row_index, col_index]).astype(jnp.int32)
    result = finish(where, panel, matrix, inverse, lower, high, low, row_count, col_count, blk)
    return result.reshape(front.shape[0], 1, blk, part_cols, 1, blk)


def solution(mesh):
    return jax.shard_map(
        body,
        mesh=mesh,
        in_specs=(
            P(None, "row", None, None, "col", None),
            P(None, None, "row", None, None, "col", None),
            P(),
        ),
        out_specs=P(None, "row", None, None, "col", None),
        check_vma=False,
    )
```

time: 1150 us -> 632 us (0.55)
  other arithmetic: 259 us -> 1.82 us
  Pallas kernels: 0 us -> 212 us
  matrix products: 168 us -> 0 us
  waiting for transfers between devices: 543 us -> 384 us
  local copies, waits for them, and re-layouts: 139 us -> 15.3 us
    psum x2 -> x0, waiting for transfers between devices: 309 us -> none  [broadcast(): return lax.psum(kept, axis)]
    ppermute x0 -> x3, waiting for transfers between devices: none -> 268 us  [body(): received.append(lax.ppermute(outgoing[turn - 1], 'col', pairs))]
    another operation x41 -> x2, other arithmetic: 243 us -> 0.58 us  [the longest x1 0.58 us: body(): where = jnp.stack([row_index, col_index]).astype(jnp.int32)]
    all_to_all x2 -> x0, waiting for transfers between devices: 217 us -> none  [the longest x1 110 us: body(): lax.all_to_all(outgoing[1], 'col', split_axis=0, concat_axis=0, tiled=True)]
    pallas_call x0 -> x5, Pallas kernels: none -> 212 us  [the longest x1 128 us: factorize(): pl.pallas_call(functools.partial(factor_kernel, blk), out_shape=[shape, s...]
    dot_general x12 -> x0, matrix products: 145 us -> none  [the longest x6 61.3 us: product(): jnp.dot(left_side, right_side, precision=highest, preferred_element_type=...]
    all_gather x4, waiting for transfers between devices: 16.9 us -> 116 us  [the longest x2 70.4 us: gather_top(): return lax.all_gather(piece, 'row', axis=0, tiled=True)]
    another operation x37 -> x1, local copies, waits for them, and re-layouts: 27.4 us -> 0.09 us  [tables(): place = jnp.stack([kind, order], axis=2).reshape(-1)]
  transfers between devices with their start and end apart: 8 -> 7, of which waited for: 6 -> 6; matrix products, arithmetic and copies ran while one was open for 35% -> 1% of each run, Pallas kernels for 0% -> 20%
where the time goes in v1:
time: 632 us; the launch traced here: 631 us
  waiting for transfers between devices  384 us (61%)
  Pallas kernels  212 us (34%)
  local copies, waits for them, and re-layouts  15.3 us (2%)
  between operations  13.2 us (2%)
    ppermute x3, waiting for transfers between devices, body(): received.append(lax.ppermute(outgoing[turn - 1], 'col', pairs))  268 us
    pallas_call x1, Pallas kernels, factorize(): pl.pallas_call(functools.partial(factor_kernel, blk), out_shape=[shape, s...  128 us
    all_gather x2, waiting for transfers between devices, gather_top(): return lax.all_gather(piece, 'row', axis=0, tiled=True)  70.4 us
    all_gather x2, waiting for transfers between devices, body(): lax.all_gather(matrix[:, s * blk:(s + 1) * blk], 'col', axis=1, tiled=True)  45.2 us
    pallas_call x1, Pallas kernels, finish(): pl.pallas_call(kernel, grid_spec=pltpu.PrefetchScalarGridSpec(num_scalar_...  32.5 us
    pallas_call x1, Pallas kernels, assemble(): pl.pallas_call(functools.partial(assemble_kernel, part_cols, child_cols,...  21 us
    pallas_call x1, Pallas kernels, right_side(): pl.pallas_call(right_kernel, grid=((cols - skip) // tile,), in_specs=[pl....  17.1 us
    pallas_call x1, Pallas kernels, pack(): pl.pallas_call(functools.partial(pack_kernel, child_cols, cap, blk), grid...  13.9 us
  transfers between devices with their start and end apart: 7, of which 6 were waited for; matrix products, arithmetic and copies ran while one was open for 1% of the time, Pallas kernels for 20%

profile of v1, /device:TPU:0, one launch (start us, length us, event | category | flops | bytes accessed | tf_op | source)
XLA Modules:
  0.0 631.2 jit_solution(5624046739337752447)
XLA Ops:
  6.5 0.0 all-gather.5.cloned.1.call-start
  6.5 0.8 slice.15
  7.3 0.1 copy.8
  7.4 0.4 fusion.1
  7.8 0.1 copy.11
  7.9 0.3 select_reduce_fusion
  8.2 0.1 copy.12
  8.3 0.6 reshape.120.table
  8.9 0.0 copy-start
  8.9 13.9 %pack.1 = (f32[12,1024,128]{2,1,0:T(8,128)}, f32[12,1024,128]{2,1,0:T(8,128)}, f32[12,1024,128]{2,1,0:T(8,128)}) custom-call(s32[48]{0:T(128)} %reshape.120.table, f32[2,8,1536,128]{3,2,1,0:T(8,128)} %bitcast.17), custom_call_target="tpu_custom_call" | custom-call | tf_op jit(solution)/shard_map/pack/pallas_call | solution.py:55
  22.8 0.5 collective-permute-start
  23.2 2.5 collective-permute-start.1
  25.8 1.4 collective-permute-start.2
  27.2 0.1 broadcast_in_dim.69
  27.3 0.0 copy-done
  27.3 0.2 compare_reduce_fusion
  27.5 0.2 fusion
  27.7 0.1 select_reduce_fusion.1
  27.8 0.1 bitcast_select_fusion
  27.9 0.1 copy.10
  28.0 0.7 reshape.118.table
  28.7 132.1 %collective-permute-done.refs_0_ = f32[12,1024,128]{2,1,0:T(8,128)} collective-permute-done((f32[12,1024,128]{2,1,0:T(8,128)}, f32[12,1024,128]{2,1,0:T(8,128)}, u32[]{:S(2)}, u32[]{:S(2)}) %collective-permute-start) | collective-permute-done | bytes 6291488 | tf_op jit(solution)/shard_map/ppermute | solution.py:357
  160.7 1.7 collective-permute-done.1.refs_1_
  162.4 133.8 %collective-permute-done.2.refs_2_ = f32[12,1024,128]{2,1,0:T(8,128)} collective-permute-done((f32[12,1024,128]{2,1,0:T(8,128)}, f32[12,1024,128]{2,1,0:T(8,128)}, u32[]{:S(2)}, u32[]{:S(2)}) %collective-permute-start.2) | collective-permute-done | bytes 6291488 | tf_op jit(solution)/shard_map/ppermute | solution.py:357
  296.2 21.0 %assemble.1.refs_1_ = f32[1024,2048]{1,0:T(8,128)} custom-call(s32[64]{0:T(128)} %reshape.118.table, f32[8,2048,128]{2,1,0:T(8,128)} %bitcast.19, f32[2,8,1536,128]{3,2,1,0:T(8,128)} %bitcast.18, f32[12,1024,128]{2,1,0:T(8,128)} %collective-permute-done.refs_0_, f32[12,1024,128]{2,1,0:T(8,128)} %collective-permute-done.1.refs_1_, ...), custom_call_target="tpu_custom_call" | custom-call | tf_op jit(solution)/shard_map/assemble/pallas_call | solution.py:93
  317.2 2.3 fusion.3
  319.5 0.0 all-gather.5.cloned.1.call-update
  319.5 0.0 all-gather.7.cloned.1.call-start
  319.6 0.7 all-gather.7.cloned.1.call-update
  320.3 0.0 all-gather.9.cloned.1.call-start
  320.3 23.9 %all-gather.5.cloned.1.call-done = f32[1024,512]{1,0:T(8,128)} async-done(((f32[1024,128]{1,0:T(8,128)}), f32[1024,512]{1,0:T(8,128)}) %all-gather.5.cloned.1.call-update) | async-done | bytes 2097168 | tf_op jit(solution)/shard_map/all_gather | solution.py:361
  344.2 3.1 constant_dynamic-update-slice_fusion.1
  347.3 21.3 %all-gather.7.cloned.1.call-done = f32[1024,512]{1,0:T(8,128)} async-done(((f32[1024,128]{1,0:T(8,128)}), f32[1024,512]{1,0:T(8,128)}) %all-gather.7.cloned.1.call-update) | async-done | bytes 2097168 | tf_op jit(solution)/shard_map/all_gather | solution.py:361
  368.6 3.1 constant_dynamic-update-slice_fusion.refs_0_
  371.8 1.9 slice.22
  373.7 0.0 all-gather.9.cloned.1.call-update
  373.7 0.2 all-gather.11.cloned.1.call-start
  373.9 2.3 slice.23
  376.2 0.0 all-gather.11.cloned.1.call-update
  376.2 0.6 pad_add_fusion.1.place
  376.8 70.4 %all-gather.9.cloned.1.call-done.square_ref = f32[1024,1024]{1,0:T(8,128)} async-done(((f32[128,1024]{1,0:T(8,128)}), f32[1024,1024]{1,0:T(8,128)}) %all-gather.9.cloned.1.call-update) | async-done | bytes 4194320 | tf_op jit(solution)/shard_map/all_gather | solution.py:336
  447.3 127.9 %factorize.1 = (f32[1024,1024]{1,0:T(8,128)}, f32[1024,1024]{1,0:T(8,128)}) custom-call(f32[1024,1024]{1,0:T(8,128)} %all-gather.9.cloned.1.call-done.square_ref), custom_call_target="tpu_custom_call" | custom-call | tf_op jit(solution)/shard_map/factorize/pallas_call | solution.py:191
  575.1 0.0 all-gather.11.cloned.1.call-done.top_ref
  575.1 17.1 %right.1 = (bf16[1024,1792]{1,0:T(8,128)(2,1)}, bf16[1024,1792]{1,0:T(8,128)(2,1)}) custom-call(f32[1024,1024]{1,0:T(8,128)} %get-tuple-element.15.inverse_ref.refs_2_, f32[1024,2048]{1,0:T(8,128)} %all-gather.11.cloned.1.call-done.top_ref), custom_call_target="tpu_custom_call" | custom-call | tf_op jit(solution)/shard_map/right/pallas_call | solution.py:212
  592.2 32.5 %finish.1 = f32[8,2048,128]{2,1,0:T(8,128)} custom-call(s32[2]{0:T(128)} %pad_add_fusion.1.place, f32[1024,1024]{1,0:T(8,128)} %constant_dynamic-update-slice_fusion.refs_0_, f32[1024,2048]{1,0:T(8,128)} %assemble.1.refs_1_, f32[1024,1024]{1,0:T(8,128)} %get-tuple-element.15.inverse_ref.refs_2_, f32[1024,1024]{1,0:T(8,128)} %get-tuple-element.16.refs_3_, ...), custom_call_target="tpu_custom_call" | custom-call | tf_op jit(solution)/shard_map/finish/pallas_call | solution.py:282
  (10 shorter events, 0.1 us)
Async XLA Ops:
  6.5 337.7 %all-gather.5.cloned.1.call-start = ((), (), s32[]{:S(2)}) async-start(), calls=%async_computation | async-start | bytes 2621440 | tf_op jit(solution)/shard_map/all_gather | solution.py:361
  8.9 18.4 %copy-start = (s32[2,48]{1,0:T(2,128)S(1)}, s32[2,48]{1,0:T(2,128)}, u32[]{:S(2)}) copy-start(s32[2,48]{1,0:T(2,128)} %param.5) | copy-start | bytes 1156
  22.8 137.9 %collective-permute-start = (f32[12,1024,128]{2,1,0:T(8,128)}, f32[12,1024,128]{2,1,0:T(8,128)}, u32[]{:S(2)}, u32[]{:S(2)}) collective-permute-start(f32[12,1024,128]{2,1,0:T(8,128)} %get-tuple-element.12), channel_id=1, source_target_pairs={{0,1},{1,2},{2,3},{3,0},{4,5},{5,6},{6,7},{7,4},{8,9},{9,10},{10,1... | collective-permute-start | bytes 18874376 | tf_op jit(solution)/shard_map/ppermute | solution.py:357
  23.2 139.1 %collective-permute-start.1 = (f32[12,1024,128]{2,1,0:T(8,128)}, f32[12,1024,128]{2,1,0:T(8,128)}, u32[]{:S(2)}, u32[]{:S(2)}) collective-permute-start(f32[12,1024,128]{2,1,0:T(8,128)} %get-tuple-element.13), channel_id=1, source_target_pairs={{0,2},{1,3},{2,0},{3,1},{4,6},{5,7},{6,4},{7,5},{8,10},{9,11},{10,... | collective-permute-start | bytes 18874376 | tf_op jit(solution)/shard_map/ppermute | solution.py:357
  25.8 270.4 %collective-permute-start.2 = (f32[12,1024,128]{2,1,0:T(8,128)}, f32[12,1024,128]{2,1,0:T(8,128)}, u32[]{:S(2)}, u32[]{:S(2)}) collective-permute-start(f32[12,1024,128]{2,1,0:T(8,128)} %get-tuple-element.14), channel_id=1, source_target_pairs={{0,3},{1,0},{2,1},{3,2},{4,7},{5,4},{6,5},{7,6},{8,11},{9,8},{10,9... | collective-permute-start | bytes 18874376 | tf_op jit(solution)/shard_map/ppermute | solution.py:357
  319.5 49.1 %all-gather.7.cloned.1.call-start = ((), (), s32[]{:S(2)}) async-start(), calls=%async_computation.1 | async-start | bytes 2621440 | tf_op jit(solution)/shard_map/all_gather | solution.py:361
  320.3 127.0 %all-gather.9.cloned.1.call-start = ((), (), s32[]{:S(2)}) async-start(), calls=%async_computation.2 | async-start | bytes 4718592 | tf_op jit(solution)/shard_map/all_gather | solution.py:336
  373.7 201.4 %all-gather.11.cloned.1.call-start = ((), (), s32[]{:S(2)}) async-start(), calls=%async_computation.3 | async-start | bytes 9437184 | tf_op jit(solution)/shard_map/all_gather | solution.py:336
Sparse Core Ops, SparseCore 0:
  319.6 24.5 all-gather.4
  345.8 22.8 all-gather.6
  373.8 73.3 all-gather.8
  449.2 123.0 all-gather.10

commit v2 on v1

--- a/solution.py
+++ b/solution.py
@@ -49,26 +49,27 @@
                 ]
 
 
-def pack(table, updates, cap):
+def pack(table, updates, cap, begin, count):
     part_rows, blk, child_cols = updates.shape[1], updates.shape[3], updates.shape[4]
     flat = updates.reshape(2, part_rows, blk * child_cols, blk)
     return pl.pallas_call(
         functools.partial(pack_kernel, child_cols, cap, blk),
         grid_spec=pltpu.PrefetchScalarGridSpec(
             num_scalar_prefetch=1,
-            grid=(part_rows,),
-            in_specs=[pl.BlockSpec((2, 1, blk * child_cols, blk), lambda a, t: (0, a, 0, 0))],
+            grid=(count,),
+            in_specs=[
+                pl.BlockSpec((2, 1, blk * child_cols, blk), lambda a, t: (0, a + begin, 0, 0))
+            ],
             out_specs=[pl.BlockSpec((2 * cap, blk, blk), lambda a, t: (0, a, 0))] * 3,
         ),
-        out_shape=[jax.ShapeDtypeStruct((2 * cap, part_rows * blk, blk), jnp.float32)] * 3,
+        out_shape=[jax.ShapeDtypeStruct((2 * cap, count * blk, blk), jnp.float32)] * 3,
         compiler_params=pltpu.CompilerParams(vmem_limit_bytes=VMEM_LIMIT),
         name="pack",
     )(table, flat)
 
 
-def assemble_kernel(part_cols, child_cols, blk, table, front_ref, updates_ref, *refs):
-    received, out_ref = refs[:3], refs[3]
-    for slot in range(part_cols):
+def add_children(out_ref, table, front_ref, updates_ref, received, slots, part_cols, child_cols, blk):
+    for slot in slots:
         cols = slice(slot * blk, (slot + 1) * blk)
         out_ref[:, cols] = front_ref[0, pl.ds(slot, blk, stride=part_cols), :]
         for member in range(2):
@@ -86,23 +87,30 @@
                     out_ref[:, cols] += received[step][index]
 
 
-def assemble(table, front, updates, received):
+def assemble(table, front, updates, received, begin, count, width):
     part_rows, blk, part_cols = front.shape[0], front.shape[2], front.shape[3]
     child_cols = updates.shape[4]
     slots = received[0].shape[0]
+
+    def kernel(table, front_ref, updates_ref, one, two, three, out_ref):
+        add_children(
+            out_ref, table, front_ref, updates_ref, (one, two, three),
+            range(width), part_cols, child_cols, blk,
+        )
+
     return pl.pallas_call(
-        functools.partial(assemble_kernel, part_cols, child_cols, blk),
+        kernel,
         grid_spec=pltpu.PrefetchScalarGridSpec(
             num_scalar_prefetch=1,
-            grid=(part_rows,),
+            grid=(count,),
             in_specs=[
-                pl.BlockSpec((1, blk * part_cols, blk), lambda a, t: (a, 0, 0)),
-                pl.BlockSpec((2, 1, blk * child_cols, blk), lambda a, t: (0, a, 0, 0)),
+                pl.BlockSpec((1, blk * part_cols, blk), lambda a, t: (a + begin, 0, 0)),
+                pl.BlockSpec((2, 1, blk * child_cols, blk), lambda a, t: (0, a + begin, 0, 0)),
             ]
             + [pl.BlockSpec((slots, blk, blk), lambda a, t: (0, a, 0))] * 3,
-            out_specs=pl.BlockSpec((blk, part_cols * blk), lambda a, t: (a, 0)),
+            out_specs=pl.BlockSpec((blk, width * blk), lambda a, t: (a, 0)),
         ),
-        out_shape=jax.ShapeDtypeStruct((part_rows * blk, part_cols * blk), jnp.float32),
+        out_shape=jax.ShapeDtypeStruct((count * blk, width * blk), jnp.float32),
         compiler_params=pltpu.CompilerParams(vmem_limit_bytes=VMEM_LIMIT),
         name="assemble",
     )(
@@ -193,6 +201,7 @@
         out_shape=[shape, shape],
         scratch_shapes=[pltpu.VMEM((size, size), jnp.float32)],
         compiler_params=pltpu.CompilerParams(vmem_limit_bytes=VMEM_LIMIT),
+        cost_estimate=pl.CostEstimate(flops=size, bytes_accessed=size, transcendentals=0),
         name="factorize",
     )(square)
 
@@ -206,15 +215,15 @@
     high_ref[...], low_ref[...] = split(result)
 
 
-def right_side(inverse, top, skip, tile):
+def right_side(inverse, top, tile):
     size, cols = top.shape
-    out = jax.ShapeDtypeStruct((size, cols - skip), jnp.bfloat16)
+    out = jax.ShapeDtypeStruct((size, cols), jnp.bfloat16)
     return pl.pallas_call(
         right_kernel,
-        grid=((cols - skip) // tile,),
+        grid=(cols // tile,),
         in_specs=[
             pl.BlockSpec((size, size), lambda n: (0, 0)),
-            pl.BlockSpec((size, tile), lambda n: (0, n + skip // tile)),
+            pl.BlockSpec((size, tile), lambda n: (0, n)),
         ],
         out_specs=[pl.BlockSpec((size, tile), lambda n: (0, n))] * 2,
         out_shape=[out, out],
@@ -224,85 +233,105 @@
     )(inverse, top)
 
 
-def final_kernel(
-    part_cols, blk, row_count, col_count, place,
-    panel_ref, matrix_ref, inverse_ref, lower_ref, high_ref, low_ref,
-    out_ref, inv_high, inv_low, left_ref,
+def finish_kernel(
+    part_cols, child_cols, blk, row_count, col_count, first, table, place,
+    panel_ref, front_ref, updates_ref, one, two, three, inverse_ref, lower_ref, high_ref, low_ref,
+    out_ref, inv_high, inv_low, left_ref, sum_ref,
 ):
     step = pl.program_id(0)
-    row_blocks = out_ref.shape[0]
+    block_row = step * row_count + place[0]
     panel_blocks = NP * col_count
+    inside = block_row < panel_blocks
+    columns = [pl.multiple_of((s * col_count + place[1]) * blk, blk) for s in range(NP)]
 
     @pl.when(step == 0)
     def _():
         inv_high[...], inv_low[...] = split(inverse_ref[...])
 
-    left_ref[...] = product3(split(panel_ref[...]), (inv_high[...], inv_low[...]), True)
-    left_pair = split(left_ref[...])
-    for pair in range(NP, part_cols, 2):
-        cols = slice((pair - NP) * blk, (pair - NP + 2) * blk)
-        trailing = product3(left_pair, (high_ref[:, cols], low_ref[:, cols]))
-        updated = matrix_ref[:, pair * blk : (pair + 2) * blk] - trailing
-        for t in range(row_blocks):
+    @pl.when(jnp.logical_not(inside))
+    def _():
+        add_children(
+            sum_ref, table, front_ref, updates_ref, (one, two, three),
+            range(NP, part_cols), part_cols, child_cols, blk,
+        )
+        panel = jnp.concatenate(
+            [
+                panel_ref[c, :, s * blk : (s + 1) * blk]
+                for s in range(NP)
+                for c in range(col_count)
+            ],
+            axis=1,
+        )
+        left_ref[...] = product3(split(panel), (inv_high[...], inv_low[...]), True)
+        left_pair = split(left_ref[...])
+        for pair in range(NP, part_cols, 2):
+            cols = slice((pair - NP) * blk, (pair - NP + 2) * blk)
+            trailing = product3(left_pair, (high_ref[:, cols], low_ref[:, cols]))
+            updated = sum_ref[:, pair * blk : (pair + 2) * blk] - trailing
             for half in range(2):
-                out_ref[t, pl.ds(pair + half, blk, stride=part_cols), :] = updated[
-                    t * blk : (t + 1) * blk, half * blk : (half + 1) * blk
+                out_ref[0, pl.ds(pair + half, blk, stride=part_cols), :] = updated[
+                    :, half * blk : (half + 1) * blk
                 ]
-    for t in range(row_blocks):
-        block_row = (step * row_blocks + t) * row_count + place[0]
-        for slot in range(NP):
-            start = pl.multiple_of((slot * col_count + place[1]) * blk, blk)
-            out_ref[t, pl.ds(slot, blk, stride=part_cols), :] = left_ref[
-                t * blk : (t + 1) * blk, pl.ds(start, blk)
+        for s in range(NP):
+            out_ref[0, pl.ds(s, blk, stride=part_cols), :] = left_ref[:, pl.ds(columns[s], blk)]
+
+    @pl.when(inside)
+    def _():
+        out_ref[...] = jnp.zeros_like(out_ref)
+        begin = pl.multiple_of(block_row * blk, blk)
+        for s in range(NP):
+            out_ref[0, pl.ds(s, blk, stride=part_cols), :] = lower_ref[
+                pl.ds(begin, blk), pl.ds(columns[s], blk)
             ]
 
-        @pl.when(block_row < panel_blocks)
-        def _():
-            out_ref[t] = jnp.zeros_like(out_ref[t])
-            begin = pl.multiple_of(block_row * blk, blk)
-            for slot in range(NP):
-                start = pl.multiple_of((slot * col_count + place[1]) * blk, blk)
-                out_ref[t, pl.ds(slot, blk, stride=part_cols), :] = lower_ref[
-                    pl.ds(begin, blk), pl.ds(start, blk)
-                ]
-
-
-def finish(place, panel, matrix, inverse, lower, high, low, row_count, col_count, blk):
-    rows, cols = matrix.shape
-    part_rows, part_cols = rows // blk, cols // blk
+
+def finish(table, place, panel, front, updates, received, inverse, lower, high, low, row_count, first):
+    part_rows, blk, part_cols = front.shape[0], front.shape[2], front.shape[3]
+    child_cols = updates.shape[4]
     size = inverse.shape[0]
-    group = 2 if part_rows % 2 == 0 else 1
+    slots = received[0].shape[0]
+    col_count = panel.shape[0]
 
     def resident(shape):
-        return pl.BlockSpec(shape, lambda a, t: (0, 0), pipeline_mode=pl.Buffered(1))
-
-    def kernel(place, *refs):
-        final_kernel(part_cols, blk, row_count, col_count, place, *refs)
+        return pl.BlockSpec(shape, lambda a, t, p: (0, 0), pipeline_mode=pl.Buffered(1))
+
+    def late(a, t, p):
+        return (0, jnp.maximum(a - first, 0), 0)
 
     return pl.pallas_call(
-        kernel,
+        functools.partial(finish_kernel, part_cols, child_cols, blk, row_count, col_count, first),
         grid_spec=pltpu.PrefetchScalarGridSpec(
-            num_scalar_prefetch=1,
-            grid=(part_rows // group,),
+            num_scalar_prefetch=2,
+            grid=(part_rows,),
             in_specs=[
-                pl.BlockSpec((group * blk, size), lambda a, t: (a, 0)),
-                pl.BlockSpec((group * blk, cols), lambda a, t: (a, 0)),
+                pl.BlockSpec((col_count, blk, NP * blk), late),
+                pl.BlockSpec((1, blk * part_cols, blk), lambda a, t, p: (a, 0, 0)),
+                pl.BlockSpec((2, 1, blk * child_cols, blk), lambda a, t, p: (0, a, 0, 0)),
+            ]
+            + [pl.BlockSpec((slots, blk, blk), late)] * 3
+            + [
                 resident((size, size)),
                 resident((size, size)),
                 resident(high.shape),
                 resident(low.shape),
             ],
-            out_specs=pl.BlockSpec((group, blk * part_cols, blk), lambda a, t: (a, 0, 0)),
+            out_specs=pl.BlockSpec((1, blk * part_cols, blk), lambda a, t, p: (a, 0, 0)),
             scratch_shapes=[
                 pltpu.VMEM((size, size), jnp.bfloat16),
                 pltpu.VMEM((size, size), jnp.bfloat16),
-                pltpu.VMEM((group * blk, size), jnp.float32),
+                pltpu.VMEM((blk, size), jnp.float32),
+                pltpu.VMEM((blk, part_cols * blk), jnp.float32),
             ],
         ),
         out_shape=jax.ShapeDtypeStruct((part_rows, blk * part_cols, blk), jnp.float32),
         compiler_params=pltpu.CompilerParams(vmem_limit_bytes=VMEM_LIMIT),
         name="finish",
-    )(place, panel, matrix, inverse, lower, high, low)
+    )(
+        table, place, panel,
+        front.reshape(part_rows, blk * part_cols, blk),
+        updates.reshape(2, part_rows, blk * child_cols, blk),
+        *received, inverse, lower, high, low,
+    )
 
 
 def tables(maps, col_index, col_count, child_cols, part_cols, cap):
@@ -350,25 +379,45 @@
     cap = child_cols // 2
     panel_blocks = NP * col_count
     send, place = tables(maps, col_index, col_count, child_cols, part_cols, cap)
-    outgoing = pack(send, updates, cap)
-    received = []
-    for turn in range(1, col_count):
-        pairs = [(c, (c + turn) % col_count) for c in range(col_count)]
-        received.append(lax.ppermute(outgoing[turn - 1], "col", pairs))
-    matrix = assemble(place, front, updates, received)
-    panel = jnp.concatenate(
+    part_rows = front.shape[0]
+    first = 1 if part_rows > 1 and row_count == panel_blocks else part_rows
+
+    def exchange(outgoing):
+        return [
+            lax.ppermute(
+                outgoing[turn - 1], "col", [(c, (c + turn) % col_count) for c in range(col_count)]
+            )
+            for turn in range(1, col_count)
+        ]
+
+    early = exchange(pack(send, updates, cap, 0, first))
+    if first < part_rows:
+        outgoing = pack(send, updates, cap, first, part_rows - first)
+        early, outgoing = lax.optimization_barrier((early, outgoing))
+        received = exchange(outgoing)
+    else:
+        received = early
+    head = assemble(place, front, updates, early, 0, 1, part_cols)
+    square = jnp.concatenate(
         [
-            lax.all_gather(matrix[:, s * blk : (s + 1) * blk], "col", axis=1, tiled=True)
+            lax.all_gather(head[:, s * blk : (s + 1) * blk], "col", axis=1, tiled=True)
             for s in range(NP)
         ],
         axis=1,
     )
-    top = gather_top(matrix[:blk], row_count, row_index, panel_blocks)
-    square = gather_top(panel[:blk], row_count, row_index, panel_blocks)
+    square = gather_top(square, row_count, row_index, panel_blocks)
+    rest, square = lax.optimization_barrier((head[:, NP * blk :], square))
+    top = gather_top(rest, row_count, row_index, panel_blocks)
     lower, inverse = factorize(square, blk)
-    high, low = right_side(inverse, top, NP * blk, 2 * blk)
+    high, low = right_side(inverse, top, 2 * blk)
+    received, high, low = lax.optimization_barrier((received, high, low))
+    late = first if first < part_rows else 0
+    panel = assemble(place, front, updates, received, late, part_rows - late, NP)
+    panel = lax.all_gather(panel, "col", axis=0)
     where = jnp.stack([row_index, col_index]).astype(jnp.int32)
-    result = finish(where, panel, matrix, inverse, lower, high, low, row_count, col_count, blk)
+    result = finish(
+        place, where, panel, front, updates, received, inverse, lower, high, low, row_count, late
+    )
     return result.reshape(front.shape[0], 1, blk, part_cols, 1, blk)
 
 

time: 632 us -> 482 us (0.76)
  waiting for transfers between devices: 384 us -> 211 us
  Pallas kernels: 212 us -> 229 us
  blocking collectives: 0 us -> 11.8 us
  local copies, waits for them, and re-layouts: 15.3 us -> 6.53 us
    ppermute x3 -> x6, waiting for transfers between devices: 268 us -> 109 us  [exchange(): lax.ppermute(outgoing[turn - 1], 'col', [(c, (c + turn) % col_count) for...]
    all_gather x2 -> x1, waiting for transfers between devices: 45.2 us -> 29.8 us  [body(): panel = lax.all_gather(panel, 'col', axis=0)]
    pallas_call x3 -> x4, Pallas kernels: 70.6 us -> 84.1 us  [the longest x1 48.7 us: finish(): pl.pallas_call(functools.partial(finish_kernel, part_cols, child_cols, bl...]
    all_gather x0 -> x2, blocking collectives: none -> 11.8 us  [body(): lax.all_gather(head[:, s * blk:(s + 1) * blk], 'col', axis=1, tiled=True)]
    pallas_call x1 -> x2, Pallas kernels: 13.9 us -> 16.7 us  [pack(): pl.pallas_call(functools.partial(pack_kernel, child_cols, cap, blk), grid...]
  transfers between devices with their start and end apart: 7 -> 9, of which waited for: 6 -> 6; matrix products, arithmetic and copies ran while one was open for 1% -> 1% of each run, Pallas kernels for 20% -> 33%
where the time goes in v2:
time: 482 us; the launch traced here: 481 us
  Pallas kernels  229 us (48%)
  waiting for transfers between devices  211 us (44%)
  between operations  13.2 us (3%)
  blocking collectives  11.8 us (2%)
  starting transfers between devices  7.46 us (2%)
  local copies, waits for them, and re-layouts  6.53 us (1%)
    pallas_call x1, Pallas kernels, factorize(): pl.pallas_call(functools.partial(factor_kernel, blk), out_shape=[shape, s...  128 us
    ppermute x6, waiting for transfers between devices, exchange(): lax.ppermute(outgoing[turn - 1], 'col', [(c, (c + turn) % col_count) for...  109 us
    all_gather x2, waiting for transfers between devices, gather_top(): return lax.all_gather(piece, 'row', axis=0, tiled=True)  71.9 us
    pallas_call x1, Pallas kernels, finish(): pl.pallas_call(functools.partial(finish_kernel, part_cols, child_cols, bl...  48.7 us
    all_gather x1, waiting for transfers between devices, body(): panel = lax.all_gather(panel, 'col', axis=0)  29.8 us
    pallas_call x2, Pallas kernels, assemble(): pl.pallas_call(kernel, grid_spec=pltpu.PrefetchScalarGridSpec(num_scalar_...  18.4 us
    pallas_call x1, Pallas kernels, right_side(): pl.pallas_call(right_kernel, grid=(cols // tile,), in_specs=[pl.BlockSpec...  17 us
    pallas_call x2, Pallas kernels, pack(): pl.pallas_call(functools.partial(pack_kernel, child_cols, cap, blk), grid...  16.7 us
  transfers between devices with their start and end apart: 9, of which 6 were waited for; matrix products, arithmetic and copies ran while one was open for 1% of the time, Pallas kernels for 33%

profile of v2, /device:TPU:0, one launch (start us, length us, event | category | flops | bytes accessed | tf_op | source)
XLA Modules:
  0.0 481.2 jit_solution(8963974562635993306)
XLA Ops:
  6.5 0.0 all-gather.5.cloned.1.call-start
  6.5 0.8 slice.12
  7.3 0.1 copy.8
  7.4 0.3 fusion.1
  7.8 0.1 copy.11
  7.9 0.3 select_reduce_fusion
  8.2 0.1 copy.12
  8.3 0.7 reshape.123.table
  8.9 3.8 pack.2
  12.8 0.5 collective-permute-start
  13.2 2.5 collective-permute-start.1
  15.7 1.4 collective-permute-start.2
  17.2 0.0 copy-start.3
  17.2 12.9 %pack.3 = (f32[12,896,128]{2,1,0:T(8,128)}, f32[12,896,128]{2,1,0:T(8,128)}, f32[12,896,128]{2,1,0:T(8,128)}) custom-call(s32[48]{0:T(128)} %reshape.123.table, f32[2,8,1536,128]{3,2,1,0:T(8,128)} %bitcast.19), custom_call_target="tpu_custom_call" | custom-call | tf_op jit(solution)/shard_map/pack/pallas_call | solution.py:55
  30.1 0.0 copy-done.3
  30.1 0.2 compare_reduce_fusion
  30.3 0.1 broadcast_in_dim.69
  30.4 0.2 fusion
  30.6 0.1 select_reduce_fusion.1
  30.7 0.1 bitcast_select_fusion
  30.8 0.1 copy.10
  30.9 0.7 reshape.121.table
  31.5 1.1 collective-permute-done.one
  32.6 0.0 copy-start
  32.6 1.7 collective-permute-done.1.two
  34.3 0.0 copy-start.1
  34.3 15.9 %collective-permute-done.2.three = f32[12,128,128]{2,1,0:T(8,128)S(1)} collective-permute-done((f32[12,128,128]{2,1,0:T(8,128)}, f32[12,128,128]{2,1,0:T(8,128)S(1)}, u32[]{:S(2)}, u32[]{:S(2)}) %collective-permute-start.2) | collective-permute-done | bytes 786464 | tf_op jit(solution)/shard_map/ppermute | solution.py:387
  50.2 0.0 copy-start.2
  50.2 0.0 copy-done
  50.2 0.0 copy-done.1
  50.2 0.9 copy-done.2
  51.1 5.4 %assemble.2 = f32[128,2048]{1,0:T(8,128)} custom-call(s32[64]{0:T(128)} %reshape.121.table, f32[8,2048,128]{2,1,0:T(8,128)} %bitcast.23, f32[2,8,1536,128]{3,2,1,0:T(8,128)} %bitcast.20, f32[12,128,128]{2,1,0:T(8,128)} %copy-done, f32[12,128,128]{2,1,0:T(8,128)} %copy-done.1, f32[12,128,128]{2,1,0:T(8,128)} %copy-done.2), custom_call_target="tpu_custom_call" | custom-call | tf_op jit(solution)/shard_map/assemble/pallas_call | solution.py:101
  56.5 0.9 fusion.3
  57.4 6.0 %all_gather.18 = f32[128,512]{1,0:T(8,128)S(1)} all-gather(f32[128,128]{1,0:T(8,128)S(1)} %get-tuple-element.53), channel_id=1, replica_groups=mesh['row'=8,'col'=4] {'col'}, dimensions={1}, use_global_device_ids=true | all-gather | bytes 327680 | tf_op jit(solution)/shard_map/all_gather | solution.py:403
  63.4 5.8 %all_gather.19 = f32[128,512]{1,0:T(8,128)S(1)} all-gather(f32[128,128]{1,0:T(8,128)S(1)} %get-tuple-element.54), channel_id=1, replica_groups=mesh['row'=8,'col'=4] {'col'}, dimensions={1}, use_global_device_ids=true | all-gather | bytes 327680 | tf_op jit(solution)/shard_map/all_gather | solution.py:403
  69.3 0.8 pad_maximum_fusion
  70.1 0.0 all-gather.5.cloned.1.call-update
  70.1 0.0 all-gather.7.cloned.1.call-start
  70.2 2.2 slice.16
  72.4 71.9 %all-gather.5.cloned.1.call-done.square_ref = f32[1024,1024]{1,0:T(8,128)} async-done(((f32[128,1024]{1,0:T(8,128)}), f32[1024,1024]{1,0:T(8,128)}) %all-gather.5.cloned.1.call-update) | async-done | bytes 4194320 | tf_op jit(solution)/shard_map/all_gather | solution.py:365
  144.3 0.0 all-gather.7.cloned.1.call-update
  144.3 0.0 all-gather.9.cloned.1.call-start
  144.4 0.1 collective-permute-start.3
  144.4 1.5 collective-permute-start.4
  146.0 1.4 collective-permute-start.5
  147.3 127.9 %factorize.1 = (f32[1024,1024]{1,0:T(8,128)}, f32[1024,1024]{1,0:T(8,128)}) custom-call(f32[1024,1024]{1,0:T(8,128)} %all-gather.5.cloned.1.call-done.square_ref), custom_call_target="tpu_custom_call" | custom-call | flops 1024 | bytes 1024 | tf_op jit(solution)/shard_map/factorize/pallas_call | solution.py:199
  275.2 0.0 all-gather.7.cloned.1.call-done.top_ref
  275.2 17.0 %right.1 = (bf16[1024,1792]{1,0:T(8,128)(2,1)}, bf16[1024,1792]{1,0:T(8,128)(2,1)}) custom-call(f32[1024,1024]{1,0:T(8,128)} %get-tuple-element.41.inverse_ref, f32[1024,1792]{1,0:T(8,128)} %all-gather.7.cloned.1.call-done.top_ref), custom_call_target="tpu_custom_call" | custom-call | tf_op jit(solution)/shard_map/right/pallas_call | solution.py:221
  292.2 0.0 collective-permute-done.3.one
  292.2 0.0 collective-permute-done.4.two
  292.2 90.4 %collective-permute-done.5.three = f32[12,896,128]{2,1,0:T(8,128)} collective-permute-done((f32[12,896,128]{2,1,0:T(8,128)}, f32[12,896,128]{2,1,0:T(8,128)}, u32[]{:S(2)}, u32[]{:S(2)}) %collective-permute-start.5) | collective-permute-done | bytes 5505056 | tf_op jit(solution)/shard_map/ppermute | solution.py:387
  382.6 13.0 %assemble.3 = f32[896,256]{1,0:T(8,128)} custom-call(s32[64]{0:T(128)} %reshape.121.table, f32[8,2048,128]{2,1,0:T(8,128)} %bitcast.24, f32[2,8,1536,128]{3,2,1,0:T(8,128)} %bitcast.21, f32[12,896,128]{2,1,0:T(8,128)} %collective-permute-done.3.one, f32[12,896,128]{2,1,0:T(8,128)} %collective-permute-done.4.two, f32[12,896,128]{2,1,0:T(8,128)} %collective-permute-done.5.three), custom_call_target="tpu_custom_call" | custom-call | tf_op jit(solution)/shard_map/assemble/pallas_call | solution.py:101
  395.6 0.0 all-gather.9.cloned.1.call-update
  395.6 0.6 pad_add_fusion.1.place
  396.3 29.8 %all-gather.9.cloned.1.call-done = f32[3584,256]{1,0:T(8,128)} async-done(((f32[896,256]{1,0:T(8,128)}), f32[3584,256]{1,0:T(8,128)}) %all-gather.9.cloned.1.call-update) | async-done | bytes 3670032 | tf_op jit(solution)/shard_map/all_gather | solution.py:416
  426.0 48.7 %finish.1 = f32[8,2048,128]{2,1,0:T(8,128)} custom-call(s32[64]{0:T(128)} %reshape.121.table, s32[2]{0:T(128)} %pad_add_fusion.1.place, f32[4,896,256]{2,1,0:T(8,128)} %bitcast.26, f32[8,2048,128]{2,1,0:T(8,128)} %bitcast.25, f32[2,8,1536,128]{3,2,1,0:T(8,128)} %bitcast.22, f32[12,896,128]{2,1,0:T(8,128)} %collective-permute-done.3.one, ...), custom_call_target="tpu_custom_call" | custom-call | tf_op jit(solution)/shard_map/finish/pallas_call | solution.py:301
  (10 shorter events, 0.1 us)
Async XLA Ops:
  6.5 137.8 %all-gather.5.cloned.1.call-start = ((), (), s32[]{:S(2)}) async-start(), calls=%async_computation | async-start | bytes 4718592 | tf_op jit(solution)/shard_map/all_gather | solution.py:365
  12.8 19.8 %collective-permute-start = (f32[12,128,128]{2,1,0:T(8,128)}, f32[12,128,128]{2,1,0:T(8,128)S(1)}, u32[]{:S(2)}, u32[]{:S(2)}) collective-permute-start(f32[12,128,128]{2,1,0:T(8,128)} %get-tuple-element.28), channel_id=1, source_target_pairs={{0,1},{1,2},{2,3},{3,0},{4,5},{5,6},{6,7},{7,4},{8,9},{9,10},{10,1... | collective-permute-start | bytes 2359304 | tf_op jit(solution)/shard_map/ppermute | solution.py:387
  13.2 21.1 %collective-permute-start.1 = (f32[12,128,128]{2,1,0:T(8,128)}, f32[12,128,128]{2,1,0:T(8,128)S(1)}, u32[]{:S(2)}, u32[]{:S(2)}) collective-permute-start(f32[12,128,128]{2,1,0:T(8,128)} %get-tuple-element.29), channel_id=1, source_target_pairs={{0,2},{1,3},{2,0},{3,1},{4,6},{5,7},{6,4},{7,5},{8,10},{9,11},{10,... | collective-permute-start | bytes 2359304 | tf_op jit(solution)/shard_map/ppermute | solution.py:387
  15.7 34.5 %collective-permute-start.2 = (f32[12,128,128]{2,1,0:T(8,128)}, f32[12,128,128]{2,1,0:T(8,128)S(1)}, u32[]{:S(2)}, u32[]{:S(2)}) collective-permute-start(f32[12,128,128]{2,1,0:T(8,128)} %get-tuple-element.30), channel_id=1, source_target_pairs={{0,3},{1,0},{2,1},{3,2},{4,7},{5,4},{6,5},{7,6},{8,11},{9,8},{10,9... | collective-permute-start | bytes 2359304 | tf_op jit(solution)/shard_map/ppermute | solution.py:387
  17.2 12.9 %copy-start.3 = (s32[2,48]{1,0:T(2,128)S(1)}, s32[2,48]{1,0:T(2,128)}, u32[]{:S(2)}) copy-start(s32[2,48]{1,0:T(2,128)} %param.5) | copy-start | bytes 1156
  32.6 17.6 %copy-start = (f32[12,128,128]{2,1,0:T(8,128)}, f32[12,128,128]{2,1,0:T(8,128)S(1)}, u32[]{:S(2)}) copy-start(f32[12,128,128]{2,1,0:T(8,128)S(1)} %collective-permute-done.one) | copy-start | bytes 2359300
  34.3 16.0 %copy-start.1 = (f32[12,128,128]{2,1,0:T(8,128)}, f32[12,128,128]{2,1,0:T(8,128)S(1)}, u32[]{:S(2)}) copy-start(f32[12,128,128]{2,1,0:T(8,128)S(1)} %collective-permute-done.1.two) | copy-start | bytes 2359300
  50.2 0.9 copy-start.2
  70.1 205.1 %all-gather.7.cloned.1.call-start = ((), (), s32[]{:S(2)}) async-start(), calls=%async_computation.1 | async-start | bytes 8257536 | tf_op jit(solution)/shard_map/all_gather | solution.py:365
  144.3 281.7 %all-gather.9.cloned.1.call-start = ((), (), s32[]{:S(2)}) async-start(), calls=%async_computation.2 | async-start | bytes 4587520 | tf_op jit(solution)/shard_map/all_gather | solution.py:416
  144.4 147.8 %collective-permute-start.3 = (f32[12,896,128]{2,1,0:T(8,128)}, f32[12,896,128]{2,1,0:T(8,128)}, u32[]{:S(2)}, u32[]{:S(2)}) collective-permute-start(f32[12,896,128]{2,1,0:T(8,128)} %get-tuple-element.34), channel_id=1, source_target_pairs={{0,1},{1,2},{2,3},{3,0},{4,5},{5,6},{6,7},{7,4},{8,9},{9,10},{10,1... | collective-permute-start | bytes 16515080 | tf_op jit(solution)/shard_map/ppermute | solution.py:387
  144.4 147.8 %collective-permute-start.4 = (f32[12,896,128]{2,1,0:T(8,128)}, f32[12,896,128]{2,1,0:T(8,128)}, u32[]{:S(2)}, u32[]{:S(2)}) collective-permute-start(f32[12,896,128]{2,1,0:T(8,128)} %get-tuple-element.35), channel_id=1, source_target_pairs={{0,2},{1,3},{2,0},{3,1},{4,6},{5,7},{6,4},{7,5},{8,10},{9,11},{10,... | collective-permute-start | bytes 16515080 | tf_op jit(solution)/shard_map/ppermute | solution.py:387
  146.0 236.7 %collective-permute-start.5 = (f32[12,896,128]{2,1,0:T(8,128)}, f32[12,896,128]{2,1,0:T(8,128)}, u32[]{:S(2)}, u32[]{:S(2)}) collective-permute-start(f32[12,896,128]{2,1,0:T(8,128)} %get-tuple-element.36), channel_id=1, source_target_pairs={{0,3},{1,0},{2,1},{3,2},{4,7},{5,4},{6,5},{7,6},{8,11},{9,8},{10,9... | collective-permute-start | bytes 16515080 | tf_op jit(solution)/shard_map/ppermute | solution.py:387
Sparse Core Ops, SparseCore 0:
  70.3 73.9 all-gather.4
  146.5 110.3 all-gather.6
  395.8 30.2 all-gather.8
